TPU v7x, 512 devices: a whole 4x8x8 slice. The times are simulated.
512 devices in a mesh: gx: 8 (over z_hi, core), gy: 8 (over y), gz: 8 (over x, z_lo).
Axes of the slice: x: 4, y: 8, z: 8 (z_hi: 4, z_lo: 2; z = z_hi * 2 + z_lo), core: 2. Of those that a mesh axis runs over, the one named last changes fastest.
Arguments:
- features: bfloat16 [8, 8, 8, 128, 128], P('gx', 'gy', 'gz'), may hold values from -6 to 6
- positions: float32 [8, 8, 8, 3, 128], P('gx', 'gy', 'gz'), may hold values from 0 to 1
- counts: int32 [8, 8, 8], P('gx', 'gy', 'gz'), may hold values from 1 to 128, as said below
- w_proj: bfloat16 [4, 128, 128], replicated, may hold values from -0.5 to 0.5
- w_mix: bfloat16 [128, 128], replicated, may hold values from -0.5 to 0.5
- w_long: bfloat16 [64, 128], replicated, may hold values from -0.75 to 0.75
- w_charge: bfloat16 [64, 128], replicated, may hold values from -0.5 to 0.5
- charge_bias: float32 [64], replicated, may hold values from -4 to 4
- w_energy: float32 [128], replicated, may hold values from -0.5 to 0.5
- k_filter: float32 [64, 2048], replicated, may hold values from 0.1 to 1
- k_index: int32 [3, 2048], replicated, may hold values from -6 to 6
Outputs:
- updated: bfloat16 [8, 8, 8, 128, 128], P('gx', 'gy', 'gz')
- energies: float32 [8, 8, 8, 128], P('gx', 'gy', 'gz')
- forces: float32 [8, 8, 8, 3, 128], P('gx', 'gy', 'gz')
Inputs may be any that keep to these rules, and one draw needn't show every extreme that they name: Slots 0 to counts[x,y,z] - 1 of cell (x,y,z) hold live atoms, the rest are padding; some cell holds 128 live atoms.
All inputs are finite; a program needn't handle non-finite values.
Results may differ from a plain program's by a relative error of at most 0.0068.
Values may be sent and summed in bfloat16 or wider, within the bound.
A program may use at most 64 MiB of HBM per device.

v0:
```python
import math
import jax
import jax.numpy as jnp
from jax import lax
from jax.sharding import PartitionSpec as P

CUTOFF = 0.9
GAMMAS = (1.0, 3.0, 8.0, 20.0)
PRECISE = lax.Precision.HIGHEST
CONTRACT_LAST = (((1,), (1,)), ((), ()))
CONTRACT_FIRST = (((0,), (0,)), ((), ()))


def extended(value, sides, width):
    for axis, dim in sides:
        peers, length = (lax.axis_size(axis), value.shape[dim])
        up = [(i, (i + 1) % peers) for i in range(peers)]
        down = [(j, i) for i, j in up]
        last = lax.slice_in_dim(value, length - width, length, axis=dim)
        initial = lax.slice_in_dim(value, 0, width, axis=dim)
        before = lax.ppermute(last, axis, up)
        after = lax.ppermute(initial, axis, down)
        value = jnp.concatenate([before, value, after], axis=dim)
    return value


def silu_grad(values):
    sigma = jax.nn.sigmoid(values)
    return sigma * (1.0 + values * (1.0 - sigma))


def pair_geometry(centre, others, neighbour):
    cell_shift = (
        jnp.stack([neighbour // 9, neighbour // 3 % 3, neighbour % 3]).astype(jnp.float32) - 1.0
    )
    offset_vec = others[:, None, :] + cell_shift[:, None, None] - centre[:, :, None]
    scaled = jnp.sum(offset_vec * offset_vec, axis=0) / (CUTOFF * CUTOFF)
    atom_count = centre.shape[1]
    slot_ids = jnp.arange(atom_count, dtype=jnp.int32)
    self_pair = (slot_ids[:, None] == slot_ids[None, :]) & (neighbour == 13)
    keep_mask = jnp.where(self_pair, 0.0, 1.0).astype(jnp.float32)
    envelope_base = jnp.maximum(1.0 - scaled, 0.0)
    decay_rates = jnp.asarray(GAMMAS, dtype=jnp.float32)[None, :, None]
    decay_terms = jnp.exp(-decay_rates * scaled[:, None, :]) * keep_mask[:, None, :]
    envelope = (envelope_base * envelope_base)[:, None, :]
    radial = decay_terms * envelope
    radial_slope = decay_terms * (-decay_rates * envelope - 2.0 * envelope_base[:, None, :])
    return (offset_vec, radial, radial_slope)


def phases(absolute, wave_vec, first_wave, wave_block):
    wave_part = wave_vec[:, first_wave : first_wave + wave_block]
    phase_angle = (
        absolute[0][:, None] * wave_part[0][None, :]
        + absolute[1][:, None] * wave_part[1][None, :]
        + absolute[2][:, None] * wave_part[2][None, :]
    )
    return (jnp.cos(phase_angle), jnp.sin(phase_angle))


def structure(weights_rows, absolute, wave_vec, wave_block):
    cosine_parts = []
    sine_parts = []
    for first_wave in range(0, wave_vec.shape[1], wave_block):
        cosine, sine_part = phases(absolute, wave_vec, first_wave, wave_block)
        cosine_parts.append(jnp.dot(weights_rows, cosine, precision=PRECISE))
        sine_parts.append(jnp.dot(weights_rows, sine_part, precision=PRECISE))
    return (jnp.concatenate(cosine_parts, axis=1), jnp.concatenate(sine_parts, axis=1))


def shards(
    features,
    positions,
    counts,
    w_proj,
    w_mix,
    w_long,
    w_charge,
    charge_bias,
    w_energy,
    k_filter,
    k_index,
):
    own_rows = features[0, 0, 0]
    centre = positions[0, 0, 0]
    atom_count, channels = own_rows.shape
    basis_count = w_proj.shape[0]
    waves = k_index.shape[1]
    wave_block = min(512, waves)
    grid_sizes = (lax.axis_size("gx"), lax.axis_size("gy"), lax.axis_size("gz"))
    scale_long = 4.0 / math.sqrt(atom_count * grid_sizes[0] * grid_sizes[1] * grid_sizes[2] * waves)
    cell_anchor = jnp.stack(
        [lax.axis_index("gx"), lax.axis_index("gy"), lax.axis_index("gz")]
    ).astype(jnp.float32)
    living = (jnp.arange(atom_count, dtype=jnp.int32) < counts[0, 0, 0]).astype(jnp.float32)
    masked = own_rows * living[:, None].astype(jnp.bfloat16)
    extent = jnp.asarray(grid_sizes, dtype=jnp.float32)
    wave_vec = 2.0 * math.pi * k_index.astype(jnp.float32) / extent[:, None]
    absolute = centre + cell_anchor[:, None]
    charges = (
        jax.nn.silu(
            lax.dot_general(w_charge, masked, CONTRACT_LAST, preferred_element_type=jnp.float32)
            + charge_bias[:, None]
        )
        * living[None, :]
    )
    stacked_rows = jnp.concatenate([charges, living[None, :]], axis=0)
    local_c, local_s = structure(stacked_rows, absolute, wave_vec, wave_block)
    totals = lax.psum(
        (local_c, local_s, jnp.sum(charges, axis=1), jnp.sum(living)), ("gx", "gy", "gz")
    )
    charge_mean = totals[2] / totals[3]
    neutral = (charges - charge_mean[:, None]) * living[None, :]
    row_count = charges.shape[0]
    struct_c = totals[0][:row_count] - charge_mean[:, None] * totals[0][row_count:]
    struct_s = totals[1][:row_count] - charge_mean[:, None] * totals[1][row_count:]
    near_pos = extended(positions, (("gx", 0), ("gy", 1), ("gz", 2)), 1).reshape(27, 3, atom_count)
    local_proj = jnp.einsum(
        "jc,bcd->bjd", masked, w_proj, preferred_element_type=jnp.float32
    ).astype(jnp.bfloat16)
    near_feat = extended(masked[None, None, None], (("gx", 0), ("gy", 1), ("gz", 2)), 1).reshape(
        27, atom_count, channels
    )

    def fetch_basis(neighbour):
        near_rows = lax.dynamic_index_in_dim(near_feat, neighbour, 0, keepdims=False)
        return (
            jnp.einsum("jc,bcd->bjd", near_rows, w_proj, preferred_element_type=jnp.float32)
            .astype(jnp.bfloat16)
            .reshape(basis_count * atom_count, channels)
        )

    def add_message(neighbour, message):
        others = lax.dynamic_index_in_dim(near_pos, neighbour, 0, keepdims=False)
        offset_vec, radial, radial_slope = pair_geometry(centre, others, neighbour)
        return message + jnp.dot(
            radial.astype(jnp.bfloat16).reshape(atom_count, -1),
            fetch_basis(neighbour),
            preferred_element_type=jnp.float32,
        )

    message = lax.fori_loop(0, 27, add_message, jnp.zeros((atom_count, channels), jnp.float32))
    filtered_cos = k_filter * struct_c
    filtered_sin = k_filter * struct_s
    potential = jnp.zeros(charges.shape, jnp.float32)
    for first_wave in range(0, waves, wave_block):
        cosine, sine_part = phases(absolute, wave_vec, first_wave, wave_block)
        potential = (
            potential
            + lax.dot_general(
                filtered_cos[:, first_wave : first_wave + wave_block],
                cosine,
                CONTRACT_LAST,
                precision=PRECISE,
            )
            + lax.dot_general(
                filtered_sin[:, first_wave : first_wave + wave_block],
                sine_part,
                CONTRACT_LAST,
                precision=PRECISE,
            )
        )
    potential = scale_long * potential
    pre_act = jnp.dot(
        message.astype(jnp.bfloat16), w_mix, preferred_element_type=jnp.float32
    ) + lax.dot_general(
        potential.astype(jnp.bfloat16), w_long, CONTRACT_FIRST, preferred_element_type=jnp.float32
    )
    refined = own_rows.astype(jnp.float32) + jax.nn.silu(pre_act)
    energy = living * jnp.sum(jax.nn.silu(refined) * w_energy[None, :], axis=1)
    grad_new = living[:, None] * w_energy[None, :] * silu_grad(refined)
    grad_pre = (grad_new * silu_grad(pre_act)).astype(jnp.bfloat16)
    adjoint = lax.dot_general(
        grad_pre, w_mix, CONTRACT_LAST, preferred_element_type=jnp.float32
    ).astype(jnp.bfloat16)
    pull_back = lax.dot_general(w_long, grad_pre, CONTRACT_LAST, preferred_element_type=jnp.float32)
    near_adjoint = extended(
        adjoint[None, None, None], (("gx", 0), ("gy", 1), ("gz", 2)), 1
    ).reshape(27, atom_count, channels)
    pull_c, pull_s = structure(pull_back, absolute, wave_vec, wave_block)
    back_c, back_s = lax.psum((pull_c, pull_s), ("gx", "gy", "gz"))

    def add_force(neighbour, near_force):
        others = lax.dynamic_index_in_dim(near_pos, neighbour, 0, keepdims=False)
        offset_vec, radial, radial_slope = pair_geometry(centre, others, neighbour)
        first_term = lax.dot_general(
            adjoint, fetch_basis(neighbour), CONTRACT_LAST, preferred_element_type=jnp.float32
        ).reshape(atom_count, basis_count, atom_count)
        near_rows = lax.dynamic_index_in_dim(near_adjoint, neighbour, 0, keepdims=False)
        second_term = jnp.einsum(
            "bic,jc->ibj", local_proj, near_rows, preferred_element_type=jnp.float32
        )
        strength = jnp.sum(radial_slope * (first_term + second_term), axis=1)
        return near_force + 2.0 / (CUTOFF * CUTOFF) * jnp.sum(
            strength[None, :, :] * offset_vec, axis=2
        )

    near_force = lax.fori_loop(0, 27, add_force, jnp.zeros((3, atom_count), jnp.float32))
    mixing = jnp.concatenate([pull_back, neutral], axis=0)
    weights_along = jnp.concatenate([filtered_sin, k_filter * back_s], axis=0)
    weights_across = jnp.concatenate([filtered_cos, k_filter * back_c], axis=0)
    ewald_grad = jnp.zeros((3, atom_count), jnp.float32)
    for first_wave in range(0, waves, wave_block):
        cosine, sine_part = phases(absolute, wave_vec, first_wave, wave_block)
        along_term = lax.dot_general(
            mixing,
            weights_along[:, first_wave : first_wave + wave_block],
            CONTRACT_FIRST,
            precision=PRECISE,
        )
        across_term = lax.dot_general(
            mixing,
            weights_across[:, first_wave : first_wave + wave_block],
            CONTRACT_FIRST,
            precision=PRECISE,
        )
        ewald_grad = ewald_grad + lax.dot_general(
            wave_vec[:, first_wave : first_wave + wave_block],
            cosine * along_term - sine_part * across_term,
            CONTRACT_LAST,
            precision=PRECISE,
        )
    forces = near_force - scale_long * ewald_grad
    return (
        refined.astype(jnp.bfloat16)[None, None, None],
        energy[None, None, None],
        forces[None, None, None],
    )


def solution(mesh):
    in_specs = (
        P("gx", "gy", "gz", None, None),
        P("gx", "gy", "gz", None, None),
        P("gx", "gy", "gz"),
        P(),
        P(),
        P(),
        P(),
        P(),
        P(),
        P(),
        P(),
    )
    out_specs = (
        P("gx", "gy", "gz", None, None),
        P("gx", "gy", "gz", None),
        P("gx", "gy", "gz", None, None),
    )
    return jax.shard_map(shards, mesh=mesh, in_specs=in_specs, out_specs=out_specs, check_vma=False)
```

profile of v0, /device:TPU:23, one launch (start us, length us, event | category | flops | bytes accessed | tf_op | source)
XLA Modules:
  0.0 663.8 jit_solution(11404104133226041706)
XLA Ops:
  7.2 6.4 collective-permute-start
  13.6 1.9 collective-permute-start.1
  17.1 6.6 collective-permute-start.7
  39.9 98.9 %all-reduce = (f32[64]{0:T(128)S(1)}, f32[]{:T(128)}) all-reduce(f32[64]{0:T(128)S(1)} %get-tuple-element.752, f32[]{:T(128)} %fusion.291), channel_id=1, replica_groups=mesh['gx'=8,'gy'=8,'gz'=8] {'gx','gy','gz'}, use_global_device_ids=true, to_apply=%region_5.6 | all-reduce | flops 65 | bytes 520 | tf_op jit(solution)/shard_map/psum | solution.py:109
  139.5 2.1 collective-permute-start.3
  141.6 3.5 collective-permute-start.2
  147.1 4.6 collective-permute-start.8
  151.7 1.9 collective-permute-start.5
  153.7 3.4 collective-permute-start.4
  157.1 2.8 collective-permute-start.11
  159.9 3.5 collective-permute-start.10
  163.6 2.9 collective-permute-done.11
  166.6 6.0 collective-permute-done.10
  173.3 20.3 %while.36 = (s32[]{:T(128)}, f32[128,128]{1,0:T(8,128)S(1)}, f32[27,3,128]{2,1,0:T(4,128)S(1)}, f32[1,1,1,3,128]{4,3,2,1,0:T(4,128)S(1)}, bf16[27,128,128]{2,1,0...) while((s32[]{:T(128)}, f32[128,128]{1,0:T(8,128)S(1)}, ...), condition=%wide.region_2.3_spmd.clone.clone, body=%wide.region_0.0_spmd.clone.clone.sunk | while | flops 34161064 | bytes 826287 | solution.py:142
  193.8 123.2 %all-reduce.8.cloned.1.call-done = (f32[65,2048]{1,0:T(8,128)}, f32[65,2048]{1,0:T(8,128)}) async-done(((f32[65,2048]{1,0:T(8,128)}, f32[65,2048]{1,0:T(8,128)}), (f32[65,2048]{1,0:T(8,128)}, f32[65,2048]{1,0:T(8,128)})) %all-reduce.8.cloned.1.call-update) | async-done | bytes 1064976 | tf_op jit(solution)/shard_map/psum | solution.py:109
  333.5 4.7 collective-permute-start.12
  349.9 3.4 collective-permute-start.14
  356.1 3.4 collective-permute-start.17
  359.5 2.1 collective-permute-start.16
  364.4 2.7 collective-permute-done.17
  367.0 6.8 %collective-permute-done.16 = bf16[3,3,1,128,128]{4,3,2,1,0:T(8,128)(2,1)} collective-permute-done((bf16[3,3,1,128,128]{4,3,2,1,0:T(8,128)(2,1)}, bf16[3,3,1,128,128]{4,3,2,1,0:T(8,128)(2,1)}, u32[]{:S(2)}, u32[]{:S(2)}) %collective-permute-start.16) | collective-permute-done | bytes 294944 | tf_op jit(solution)/shard_map/ppermute | solution.py:21
  373.8 2.0 pad_maximum_fusion.1
  375.8 67.3 %while.37 = (s32[]{:T(128)}, f32[3,128]{1,0:T(4,128)S(1)}, f32[27,3,128]{2,1,0:T(4,128)S(1)}, f32[1,1,1,3,128]{4,3,2,1,0:T(4,128)S(1)}, bf16[27,128,128]{2,1,0:T...) while((s32[]{:T(128)}, f32[3,128]{1,0:T(4,128)S(1)}, ...), condition=%wide.region_14.15_spmd.clone.clone, body=%wide.region_10.14_spmd.clone.clone.sunk | while | flops 51315852 | bytes 2604507 | solution.py:198
  443.1 199.9 %all-reduce.6.cloned.1.call-done = (f32[64,2048]{1,0:T(8,128)}, f32[64,2048]{1,0:T(8,128)}) async-done(((f32[64,2048]{1,0:T(8,128)}, f32[64,2048]{1,0:T(8,128)}), (f32[64,2048]{1,0:T(8,128)}, f32[64,2048]{1,0:T(8,128)})) %all-reduce.6.cloned.1.call-update) | async-done | bytes 1048592 | tf_op jit(solution)/shard_map/psum | solution.py:181
  (723 shorter events, 147.4 us)
Async XLA Ops:
  7.2 309.8 %all-reduce.8.cloned.1.call-start = ((), (), s32[]{:S(2)}) async-start(), calls=%async_computation.1 | async-start | bytes 2359296 | tf_op jit(solution)/shard_map/psum | solution.py:109
  7.2 132.2 %collective-permute-start = (f32[1,1,1,3,128]{4,2,3,1,0:T(1,128)}, f32[1,1,1,3,128]{4,2,3,1,0:T(1,128)S(1)}, u32[]{:S(2)}, u32[]{:S(2)}) collective-permute-start(f32[1,1,1,3,128]{4,2,3,1,0:T(1,128)} %param.19), channel_id=1, source_target_pairs={{0,64},{64,128},{128,192},{192,256},{256,320},{320,384},{384,448},... | collective-permute-start | bytes 4616 | tf_op jit(solution)/shard_map/ppermute | solution.py:21
  13.6 125.9 %collective-permute-start.1 = (f32[1,1,1,3,128]{4,2,3,1,0:T(1,128)}, f32[1,1,1,3,128]{4,2,3,1,0:T(1,128)S(1)}, u32[]{:S(2)}, u32[]{:S(2)}) collective-permute-start(f32[1,1,1,3,128]{4,2,3,1,0:T(1,128)} %param.19), channel_id=1, source_target_pairs={{64,0},{128,64},{192,128},{256,192},{320,256},{384,320},{448,384},... | collective-permute-start | bytes 4616 | tf_op jit(solution)/shard_map/ppermute | solution.py:22
  17.1 128.0 %collective-permute-start.7 = (bf16[1,1,1,128,128]{4,3,2,1,0:T(8,128)(2,1)S(1)}, bf16[1,1,1,128,128]{4,3,2,1,0:T(8,128)(2,1)S(1)}, u32[]{:S(2)}, u32[]{:S(2)}) collective-permute-start(bf16[1,1,1,128,128]{4,3,2,1,0:T(8,128)(2,1)S(1)} %broadcast_multiply_fusion.2), channel_id=1, source_target_pairs={{64,0},{128,64},{192,128},{256,192},{320,256},{384,320},{448,384},... | collective-permute-start | bytes 98312 | tf_op jit(solution)/shard_map/ppermute | solution.py:22
  23.7 121.4 %collective-permute-start.6 = (bf16[1,1,1,128,128]{4,3,2,1,0:T(8,128)(2,1)S(1)}, bf16[1,1,1,128,128]{4,3,2,1,0:T(8,128)(2,1)S(1)}, u32[]{:S(2)}, u32[]{:S(2)}) collective-permute-start(bf16[1,1,1,128,128]{4,3,2,1,0:T(8,128)(2,1)S(1)} %broadcast_multiply_fusion.2), channel_id=1, source_target_pairs={{0,64},{64,128},{128,192},{192,256},{256,320},{320,384},{384,448},... | collective-permute-start | bytes 98312 | tf_op jit(solution)/shard_map/ppermute | solution.py:21
  25.9 320.7 %copy-start.20 = (f32[1,512]{1,0:T(1,128)}, f32[1,512]{1,0:T(1,128)S(1)}, u32[]{:S(2)}) copy-start(f32[1,512]{1,0:T(1,128)S(1)} %get-tuple-element.744) | copy-start | bytes 6148
  26.0 320.7 %copy-start.22 = (f32[1,512]{1,0:T(1,128)}, f32[1,512]{1,0:T(1,128)S(1)}, u32[]{:S(2)}) copy-start(f32[1,512]{1,0:T(1,128)S(1)} %get-tuple-element.745) | copy-start | bytes 6148
  26.0 320.7 %copy-start.24 = (f32[1,512]{1,0:T(1,128)}, f32[1,512]{1,0:T(1,128)S(1)}, u32[]{:S(2)}) copy-start(f32[1,512]{1,0:T(1,128)S(1)} %get-tuple-element.746) | copy-start | bytes 6148
  26.8 326.5 %copy-start.5 = (f32[128]{0:T(128)}, f32[128]{0:T(128)S(1)}, u32[]{:S(2)}) copy-start(f32[128]{0:T(128)S(1)} %get-tuple-element.751) | copy-start | bytes 1540
  38.8 604.2 %all-reduce.6.cloned.1.call-start = ((), (), s32[]{:S(2)}) async-start(), calls=%async_computation | async-start | bytes 2097152 | tf_op jit(solution)/shard_map/psum | solution.py:181
  139.5 12.2 %collective-permute-start.3 = (f32[3,1,1,3,128]{4,2,3,1,0:T(1,128)S(1)}, f32[3,1,1,3,128]{4,2,3,1,0:T(1,128)S(1)}, u32[]{:S(2)}, u32[]{:S(2)}) collective-permute-start(f32[3,1,1,3,128]{4,2,3,1,0:T(1,128)S(1)} %constant_dynamic-update-slice_fusion), channel_id=1, source_target_pairs={{8,0},{16,8},{24,16},{32,24},{40,32},{48,40},{56,48},{0,56},{9,1},... | collective-permute-start | bytes 13832 | tf_op jit(solution)/shard_map/ppermute | solution.py:22
  141.6 10.1 %collective-permute-start.2 = (f32[3,1,1,3,128]{4,2,3,1,0:T(1,128)S(1)}, f32[3,1,1,3,128]{4,2,3,1,0:T(1,128)S(1)}, u32[]{:S(2)}, u32[]{:S(2)}) collective-permute-start(f32[3,1,1,3,128]{4,2,3,1,0:T(1,128)S(1)} %constant_dynamic-update-slice_fusion), channel_id=1, source_target_pairs={{0,8},{8,16},{16,24},{24,32},{32,40},{40,48},{48,56},{56,0},{1,9},... | collective-permute-start | bytes 13832 | tf_op jit(solution)/shard_map/ppermute | solution.py:21
  145.2 11.9 %collective-permute-start.9 = (bf16[3,1,1,128,128]{4,3,2,1,0:T(8,128)(2,1)S(1)}, bf16[3,1,1,128,128]{4,3,2,1,0:T(8,128)(2,1)S(1)}, u32[]{:S(2)}, u32[]{:S(2)}) collective-permute-start(bf16[3,1,1,128,128]{4,3,2,1,0:T(8,128)(2,1)S(1)} %pad_maximum_fusion.12), channel_id=1, source_target_pairs={{8,0},{16,8},{24,16},{32,24},{40,32},{48,40},{56,48},{0,56},{9,1},... | collective-permute-start | bytes 294920 | tf_op jit(solution)/shard_map/ppermute | solution.py:22
  147.1 9.9 %collective-permute-start.8 = (bf16[3,1,1,128,128]{4,3,2,1,0:T(8,128)(2,1)S(1)}, bf16[3,1,1,128,128]{4,3,2,1,0:T(8,128)(2,1)S(1)}, u32[]{:S(2)}, u32[]{:S(2)}) collective-permute-start(bf16[3,1,1,128,128]{4,3,2,1,0:T(8,128)(2,1)S(1)} %pad_maximum_fusion.12), channel_id=1, source_target_pairs={{0,8},{8,16},{16,24},{24,32},{32,40},{40,48},{48,56},{56,0},{1,9},... | collective-permute-start | bytes 294920 | tf_op jit(solution)/shard_map/ppermute | solution.py:21
  151.7 11.8 %collective-permute-start.5 = (f32[3,3,1,3,128]{4,2,3,1,0:T(1,128)S(1)}, f32[3,3,1,3,128]{4,2,3,1,0:T(1,128)S(1)}, u32[]{:S(2)}, u32[]{:S(2)}) collective-permute-start(f32[3,3,1,3,128]{4,2,3,1,0:T(1,128)S(1)} %pad_maximum_fusion.17), channel_id=1, source_target_pairs={{1,0},{2,1},{3,2},{4,3},{5,4},{6,5},{7,6},{0,7},{9,8},{10,9},{11,1... | collective-permute-start | bytes 41480 | tf_op jit(solution)/shard_map/ppermute | solution.py:22
  153.7 9.9 %collective-permute-start.4 = (f32[3,3,1,3,128]{4,2,3,1,0:T(1,128)S(1)}, f32[3,3,1,3,128]{4,2,3,1,0:T(1,128)S(1)}, u32[]{:S(2)}, u32[]{:S(2)}) collective-permute-start(f32[3,3,1,3,128]{4,2,3,1,0:T(1,128)S(1)} %pad_maximum_fusion.17), channel_id=1, source_target_pairs={{0,1},{1,2},{2,3},{3,4},{4,5},{5,6},{6,7},{7,0},{8,9},{9,10},{10,1... | collective-permute-start | bytes 41480 | tf_op jit(solution)/shard_map/ppermute | solution.py:21
  157.1 9.5 %collective-permute-start.11 = (bf16[3,3,1,128,128]{4,3,2,1,0:T(8,128)(2,1)S(1)}, bf16[3,3,1,128,128]{4,3,2,1,0:T(8,128)(2,1)S(1)}, u32[]{:S(2)}, u32[]{:S(2)}) collective-permute-start(bf16[3,3,1,128,128]{4,3,2,1,0:T(8,128)(2,1)S(1)} %pad_maximum_fusion.6), channel_id=1, source_target_pairs={{1,0},{2,1},{3,2},{4,3},{5,4},{6,5},{7,6},{0,7},{9,8},{10,9},{11,1... | collective-permute-start | bytes 884744 | tf_op jit(solution)/shard_map/ppermute | solution.py:22
  159.9 12.6 %collective-permute-start.10 = (bf16[3,3,1,128,128]{4,3,2,1,0:T(8,128)(2,1)S(1)}, bf16[3,3,1,128,128]{4,3,2,1,0:T(8,128)(2,1)S(1)}, u32[]{:S(2)}, u32[]{:S(2)}) collective-permute-start(bf16[3,3,1,128,128]{4,3,2,1,0:T(8,128)(2,1)S(1)} %pad_maximum_fusion.6), channel_id=1, source_target_pairs={{0,1},{1,2},{2,3},{3,4},{4,5},{5,6},{6,7},{7,0},{8,9},{9,10},{10,1... | collective-permute-start | bytes 884744 | tf_op jit(solution)/shard_map/ppermute | solution.py:21
  331.6 16.3 %collective-permute-start.13 = (bf16[1,1,1,128,128]{4,3,2,1,0:T(8,128)(2,1)S(1)}, bf16[1,1,1,128,128]{4,3,2,1,0:T(8,128)(2,1)S(1)}, u32[]{:S(2)}, u32[]{:S(2)}) collective-permute-start(bf16[1,1,1,128,128]{4,3,2,1,0:T(8,128)(2,1)S(1)} %bitcast.201), channel_id=1, source_target_pairs={{64,0},{128,64},{192,128},{256,192},{320,256},{384,320},{448,384},... | collective-permute-start | bytes 98312 | tf_op jit(solution)/shard_map/ppermute | solution.py:22
  333.5 14.4 %collective-permute-start.12 = (bf16[1,1,1,128,128]{4,3,2,1,0:T(8,128)(2,1)S(1)}, bf16[1,1,1,128,128]{4,3,2,1,0:T(8,128)(2,1)S(1)}, u32[]{:S(2)}, u32[]{:S(2)}) collective-permute-start(bf16[1,1,1,128,128]{4,3,2,1,0:T(8,128)(2,1)S(1)} %bitcast.202), channel_id=1, source_target_pairs={{0,64},{64,128},{128,192},{192,256},{256,320},{320,384},{384,448},... | collective-permute-start | bytes 98312 | tf_op jit(solution)/shard_map/ppermute | solution.py:21
  348.0 6.6 collective-permute-start.15
  349.9 5.4 collective-permute-start.14
  356.1 11.0 %collective-permute-start.17 = (bf16[3,3,1,128,128]{4,3,2,1,0:T(8,128)(2,1)}, bf16[3,3,1,128,128]{4,3,2,1,0:T(8,128)(2,1)S(1)}, u32[]{:S(2)}, u32[]{:S(2)}) collective-permute-start(bf16[3,3,1,128,128]{4,3,2,1,0:T(8,128)(2,1)} %pad_maximum_fusion.7), channel_id=1, source_target_pairs={{1,0},{2,1},{3,2},{4,3},{5,4},{6,5},{7,6},{0,7},{9,8},{10,9},{11,1... | collective-permute-start | bytes 884744 | tf_op jit(solution)/shard_map/ppermute | solution.py:22
  359.5 14.3 %collective-permute-start.16 = (bf16[3,3,1,128,128]{4,3,2,1,0:T(8,128)(2,1)}, bf16[3,3,1,128,128]{4,3,2,1,0:T(8,128)(2,1)}, u32[]{:S(2)}, u32[]{:S(2)}) collective-permute-start(bf16[3,3,1,128,128]{4,3,2,1,0:T(8,128)(2,1)} %pad_maximum_fusion.7), channel_id=1, source_target_pairs={{0,1},{1,2},{2,3},{3,4},{4,5},{5,6},{6,7},{7,0},{8,9},{9,10},{10,1... | collective-permute-start | bytes 884744 | tf_op jit(solution)/shard_map/ppermute | solution.py:21
  (37 other events, 3245.5 us)
Sparse Core Ops, SparseCore 0:
  38.9 278.0 all-reduce.7
  363.3 279.6 all-reduce.5
where the time goes:
time: 675 us; the launch traced here: 664 us
  waiting for transfers between devices  342 us (51%)
  blocking collectives  98.9 us (15%)
  matrix products  87.7 us (13%)
  starting transfers between devices  58.1 us (9%)
  other arithmetic  34.2 us (5%)
  local copies, waits for them, and re-layouts  18.9 us (3%)
  between operations  16.1 us (2%)
  loops' own time  7.66 us (1%)
    psum x1, waiting for transfers between devices, shards(): back_c, back_s = lax.psum((pull_c, pull_s), ('gx', 'gy', 'gz'))  200 us
    psum x1, waiting for transfers between devices, shards(): lax.psum((local_c, local_s, jnp.sum(charges, axis=1), jnp.sum(living)), (...  123 us
    psum x1, blocking collectives, shards(): lax.psum((local_c, local_s, jnp.sum(charges, axis=1), jnp.sum(living)), (...  98.9 us
    ppermute x9, starting transfers between devices, extended(): before = lax.ppermute(last, axis, up)  33.5 us
    dot_general x27, matrix products, add_force(): jnp.einsum('bic,jc->ibj', local_proj, near_rows, preferred_element_type=j...  26 us
    ppermute x9, starting transfers between devices, extended(): after = lax.ppermute(initial, axis, down)  24.6 us
    ppermute x9, waiting for transfers between devices, extended(): before = lax.ppermute(last, axis, up)  13.5 us
  transfers between devices with their start and end apart: 20, of which 7 were waited for; matrix products, arithmetic and copies ran while one was open for 16% of the time, Pallas kernels for 0%

commit v1 on v0

--- a/solution.py
+++ b/solution.py
@@ -9,6 +9,12 @@
 PRECISE = lax.Precision.HIGHEST
 CONTRACT_LAST = (((1,), (1,)), ((), ()))
 CONTRACT_FIRST = (((0,), (0,)), ((), ()))
+
+
+def clear_pools_for(u):
+    e_next = lax.psum(u, ("gy", "gz"))
+    upper = lax.psum(e_next, "gx")
+    return upper
 
 
 def extended(value, sides, width):
@@ -106,9 +112,7 @@
     )
     stacked_rows = jnp.concatenate([charges, living[None, :]], axis=0)
     local_c, local_s = structure(stacked_rows, absolute, wave_vec, wave_block)
-    totals = lax.psum(
-        (local_c, local_s, jnp.sum(charges, axis=1), jnp.sum(living)), ("gx", "gy", "gz")
-    )
+    totals = clear_pools_for((local_c, local_s, jnp.sum(charges, axis=1), jnp.sum(living)))
     charge_mean = totals[2] / totals[3]
     neutral = (charges - charge_mean[:, None]) * living[None, :]
     row_count = charges.shape[0]

time: 675 us -> 1080 us (1.60)
  waiting for transfers between devices: 342 us -> 675 us
  blocking collectives: 98.9 us -> 153 us
  starting transfers between devices: 58.1 us -> 73.8 us
    psum x1 -> x2, waiting for transfers between devices: 123 us -> 455 us  [the longest x1 344 us: clear_pools_for(): e_next = lax.psum(u, ('gy', 'gz'))]
    psum x1 -> x2, blocking collectives: 98.9 us -> 153 us  [the longest x1 114 us: clear_pools_for(): e_next = lax.psum(u, ('gy', 'gz'))]
    ppermute x9, starting transfers between devices: 33.5 us -> 49.1 us  [extended(): before = lax.ppermute(last, axis, up)]
  transfers between devices with their start and end apart: 20 -> 21, of which waited for: 7 -> 7; matrix products, arithmetic and copies ran while one was open for 16% -> 10% of each run, Pallas kernels for 0% -> 0%
where the time goes in v1:
time: 1080 us; the launch traced here: 1070 us
  waiting for transfers between devices  675 us (62%)
  blocking collectives  153 us (14%)
  matrix products  87.7 us (8%)
  starting transfers between devices  73.8 us (7%)
  other arithmetic  34.2 us (3%)
  local copies, waits for them, and re-layouts  18.9 us (2%)
  between operations  15.8 us (1%)
    psum x1, waiting for transfers between devices, clear_pools_for(): e_next = lax.psum(u, ('gy', 'gz'))  344 us
    psum x1, waiting for transfers between devices, shards(): back_c, back_s = lax.psum((pull_c, pull_s), ('gx', 'gy', 'gz'))  205 us
    psum x1, blocking collectives, clear_pools_for(): e_next = lax.psum(u, ('gy', 'gz'))  114 us
    psum x1, waiting for transfers between devices, clear_pools_for(): upper = lax.psum(e_next, 'gx')  111 us
    ppermute x9, starting transfers between devices, extended(): before = lax.ppermute(last, axis, up)  49.1 us
    psum x1, blocking collectives, clear_pools_for(): upper = lax.psum(e_next, 'gx')  39.4 us
    dot_general x27, matrix products, add_force(): jnp.einsum('bic,jc->ibj', local_proj, near_rows, preferred_element_type=j...  26 us
    ppermute x9, starting transfers between devices, extended(): after = lax.ppermute(initial, axis, down)  24.1 us
  transfers between devices with their start and end apart: 21, of which 7 were waited for; matrix products, arithmetic and copies ran while one was open for 10% of the time, Pallas kernels for 0%

profile of v1, /device:TPU:23, one launch (start us, length us, event | category | flops | bytes accessed | tf_op | source)
XLA Modules:
  0.0 1066.0 jit_solution(7272354392614518872)
XLA Ops:
  7.2 6.4 collective-permute-start
  13.6 1.9 collective-permute-start.1
  17.1 6.6 collective-permute-start.7
  39.9 113.6 %all-reduce.1 = (f32[64]{0:T(128)S(1)}, f32[]{:T(128)}) all-reduce(f32[64]{0:T(128)S(1)} %get-tuple-element.756, f32[]{:T(128)} %fusion.291), channel_id=1, replica_groups=mesh['gx'=8,'gy'=8,'gz'=8] {'gy','gz'}, use_global_device_ids=true, to_apply=%region_6.7 | all-reduce | flops 65 | bytes 520 | tf_op jit(solution)/shard_map/psum | solution.py:15
  153.5 39.4 %all-reduce.3 = (f32[64]{0:T(128)S(1)}, f32[]{:T(128)}) all-reduce(f32[64]{0:T(128)S(1)} %get-tuple-element.720, f32[]{:T(128)} %get-tuple-element.721), channel_id=1, replica_groups=mesh['gx'=8,'gy'=8,'gz'=8] {'gx'}, use_global_device_ids=true, to_apply=%region_7.8 | all-reduce | flops 65 | bytes 520 | tf_op jit(solution)/shard_map/psum | solution.py:16
  195.5 16.4 %collective-permute-start.2 = (f32[3,1,1,3,128]{4,2,3,1,0:T(1,128)S(1)}, f32[3,1,1,3,128]{4,2,3,1,0:T(1,128)S(1)}, u32[]{:S(2)}, u32[]{:S(2)}) collective-permute-start(f32[3,1,1,3,128]{4,2,3,1,0:T(1,128)S(1)} %constant_dynamic-update-slice_fusion), channel_id=1, source_target_pairs={{0,8},{8,16},{16,24},{24,32},{32,40},{40,48},{48,56},{56,0},{1,9},... | collective-permute-start | bytes 13832 | tf_op jit(solution)/shard_map/ppermute | solution.py:27
  213.9 4.6 collective-permute-start.8
  220.4 4.7 collective-permute-start.4
  227.1 5.8 collective-permute-start.10
  233.0 4.3 collective-permute-done.11
  237.3 3.5 collective-permute-done.10
  240.9 344.1 %all-reduce.11.cloned.1.call-done = (f32[65,2048]{1,0:T(8,128)}, f32[65,2048]{1,0:T(8,128)}) async-done(((f32[65,2048]{1,0:T(8,128)}, f32[65,2048]{1,0:T(8,128)}), (f32[65,2048]{1,0:T(8,128)}, f32[65,2048]{1,0:T(8,128)})) %all-reduce.11.cloned.1.call-update) | async-done | bytes 1064976 | tf_op jit(solution)/shard_map/psum | solution.py:15
  586.2 20.3 %while.36 = (s32[]{:T(128)}, f32[128,128]{1,0:T(8,128)S(1)}, f32[27,3,128]{2,1,0:T(4,128)S(1)}, f32[1,1,1,3,128]{4,3,2,1,0:T(4,128)S(1)}, bf16[27,128,128]{2,1,0...) while((s32[]{:T(128)}, f32[128,128]{1,0:T(8,128)S(1)}, ...), condition=%wide.region_2.3_spmd.clone.clone, body=%wide.region_0.0_spmd.clone.clone.sunk | while | flops 34161064 | bytes 826287 | solution.py:146
  606.7 111.3 %all-reduce.13.cloned.1.call-done = (f32[65,2048]{1,0:T(8,128)}, f32[65,2048]{1,0:T(8,128)}) async-done(((f32[65,2048]{1,0:T(8,128)}, f32[65,2048]{1,0:T(8,128)}), (f32[65,2048]{1,0:T(8,128)}, f32[65,2048]{1,0:T(8,128)})) %all-reduce.13.cloned.1.call-update) | async-done | bytes 1064976 | tf_op jit(solution)/shard_map/psum | solution.py:16
  732.6 3.2 collective-permute-start.13
  735.8 3.4 collective-permute-start.12
  749.0 2.2 collective-permute-start.15
  751.1 3.1 collective-permute-start.14
  757.3 2.6 collective-permute-start.17
  759.9 2.9 collective-permute-start.16
  765.6 6.0 collective-permute-done.16
  771.6 2.0 pad_maximum_fusion.1
  773.6 67.3 %while.37 = (s32[]{:T(128)}, f32[3,128]{1,0:T(4,128)S(1)}, f32[27,3,128]{2,1,0:T(4,128)S(1)}, f32[1,1,1,3,128]{4,3,2,1,0:T(4,128)S(1)}, bf16[27,128,128]{2,1,0:T...) while((s32[]{:T(128)}, f32[3,128]{1,0:T(4,128)S(1)}, ...), condition=%wide.region_18.19_spmd.clone.clone, body=%wide.region_14.18_spmd.clone.clone.sunk | while | flops 51315852 | bytes 2604507 | solution.py:202
  840.9 204.6 %all-reduce.9.cloned.1.call-done = (f32[64,2048]{1,0:T(8,128)}, f32[64,2048]{1,0:T(8,128)}) async-done(((f32[64,2048]{1,0:T(8,128)}, f32[64,2048]{1,0:T(8,128)}), (f32[64,2048]{1,0:T(8,128)}, f32[64,2048]{1,0:T(8,128)})) %all-reduce.9.cloned.1.call-update) | async-done | bytes 1048592 | tf_op jit(solution)/shard_map/psum | solution.py:185
  (727 shorter events, 150.1 us)
Async XLA Ops:
  7.2 577.8 %all-reduce.11.cloned.1.call-start = ((), (), s32[]{:S(2)}) async-start(), calls=%async_computation.1 | async-start | bytes 2359296 | tf_op jit(solution)/shard_map/psum | solution.py:15
  7.2 186.3 %collective-permute-start = (f32[1,1,1,3,128]{4,2,3,1,0:T(1,128)}, f32[1,1,1,3,128]{4,2,3,1,0:T(1,128)S(1)}, u32[]{:S(2)}, u32[]{:S(2)}) collective-permute-start(f32[1,1,1,3,128]{4,2,3,1,0:T(1,128)} %param.19), channel_id=1, source_target_pairs={{0,64},{64,128},{128,192},{192,256},{256,320},{320,384},{384,448},... | collective-permute-start | bytes 4616 | tf_op jit(solution)/shard_map/ppermute | solution.py:27
  13.6 180.0 %collective-permute-start.1 = (f32[1,1,1,3,128]{4,2,3,1,0:T(1,128)}, f32[1,1,1,3,128]{4,2,3,1,0:T(1,128)S(1)}, u32[]{:S(2)}, u32[]{:S(2)}) collective-permute-start(f32[1,1,1,3,128]{4,2,3,1,0:T(1,128)} %param.19), channel_id=1, source_target_pairs={{64,0},{128,64},{192,128},{256,192},{320,256},{384,320},{448,384},... | collective-permute-start | bytes 4616 | tf_op jit(solution)/shard_map/ppermute | solution.py:28
  17.1 194.8 %collective-permute-start.7 = (bf16[1,1,1,128,128]{4,3,2,1,0:T(8,128)(2,1)S(1)}, bf16[1,1,1,128,128]{4,3,2,1,0:T(8,128)(2,1)S(1)}, u32[]{:S(2)}, u32[]{:S(2)}) collective-permute-start(bf16[1,1,1,128,128]{4,3,2,1,0:T(8,128)(2,1)S(1)} %broadcast_multiply_fusion.2), channel_id=1, source_target_pairs={{64,0},{128,64},{192,128},{256,192},{320,256},{384,320},{448,384},... | collective-permute-start | bytes 98312 | tf_op jit(solution)/shard_map/ppermute | solution.py:28
  23.7 188.2 %collective-permute-start.6 = (bf16[1,1,1,128,128]{4,3,2,1,0:T(8,128)(2,1)S(1)}, bf16[1,1,1,128,128]{4,3,2,1,0:T(8,128)(2,1)S(1)}, u32[]{:S(2)}, u32[]{:S(2)}) collective-permute-start(bf16[1,1,1,128,128]{4,3,2,1,0:T(8,128)(2,1)S(1)} %broadcast_multiply_fusion.2), channel_id=1, source_target_pairs={{0,64},{64,128},{128,192},{192,256},{256,320},{320,384},{384,448},... | collective-permute-start | bytes 98312 | tf_op jit(solution)/shard_map/ppermute | solution.py:27
  25.9 721.7 %copy-start.20 = (f32[1,512]{1,0:T(1,128)}, f32[1,512]{1,0:T(1,128)S(1)}, u32[]{:S(2)}) copy-start(f32[1,512]{1,0:T(1,128)S(1)} %get-tuple-element.748) | copy-start | bytes 6148
  26.0 721.7 %copy-start.22 = (f32[1,512]{1,0:T(1,128)}, f32[1,512]{1,0:T(1,128)S(1)}, u32[]{:S(2)}) copy-start(f32[1,512]{1,0:T(1,128)S(1)} %get-tuple-element.749) | copy-start | bytes 6148
  26.8 727.5 %copy-start.5 = (f32[128]{0:T(128)}, f32[128]{0:T(128)S(1)}, u32[]{:S(2)}) copy-start(f32[128]{0:T(128)S(1)} %get-tuple-element.755) | copy-start | bytes 1540
  38.8 679.2 %all-reduce.13.cloned.1.call-start = ((), (), s32[]{:S(2)}) async-start(), calls=%async_computation.2 | async-start | bytes 2359296 | tf_op jit(solution)/shard_map/psum | solution.py:16
  193.6 24.8 %collective-permute-start.3 = (f32[3,1,1,3,128]{4,2,3,1,0:T(1,128)S(1)}, f32[3,1,1,3,128]{4,2,3,1,0:T(1,128)S(1)}, u32[]{:S(2)}, u32[]{:S(2)}) collective-permute-start(f32[3,1,1,3,128]{4,2,3,1,0:T(1,128)S(1)} %constant_dynamic-update-slice_fusion), channel_id=1, source_target_pairs={{8,0},{16,8},{24,16},{32,24},{40,32},{48,40},{56,48},{0,56},{9,1},... | collective-permute-start | bytes 13832 | tf_op jit(solution)/shard_map/ppermute | solution.py:28
  195.5 22.9 %collective-permute-start.2 = (f32[3,1,1,3,128]{4,2,3,1,0:T(1,128)S(1)}, f32[3,1,1,3,128]{4,2,3,1,0:T(1,128)S(1)}, u32[]{:S(2)}, u32[]{:S(2)}) collective-permute-start(f32[3,1,1,3,128]{4,2,3,1,0:T(1,128)S(1)} %constant_dynamic-update-slice_fusion), channel_id=1, source_target_pairs={{0,8},{8,16},{16,24},{24,32},{32,40},{40,48},{48,56},{56,0},{1,9},... | collective-permute-start | bytes 13832 | tf_op jit(solution)/shard_map/ppermute | solution.py:27
  211.9 13.1 %collective-permute-start.9 = (bf16[3,1,1,128,128]{4,3,2,1,0:T(8,128)(2,1)S(1)}, bf16[3,1,1,128,128]{4,3,2,1,0:T(8,128)(2,1)S(1)}, u32[]{:S(2)}, u32[]{:S(2)}) collective-permute-start(bf16[3,1,1,128,128]{4,3,2,1,0:T(8,128)(2,1)S(1)} %pad_maximum_fusion.12), channel_id=1, source_target_pairs={{8,0},{16,8},{24,16},{32,24},{40,32},{48,40},{56,48},{0,56},{9,1},... | collective-permute-start | bytes 294920 | tf_op jit(solution)/shard_map/ppermute | solution.py:28
  213.9 11.2 %collective-permute-start.8 = (bf16[3,1,1,128,128]{4,3,2,1,0:T(8,128)(2,1)S(1)}, bf16[3,1,1,128,128]{4,3,2,1,0:T(8,128)(2,1)S(1)}, u32[]{:S(2)}, u32[]{:S(2)}) collective-permute-start(bf16[3,1,1,128,128]{4,3,2,1,0:T(8,128)(2,1)S(1)} %pad_maximum_fusion.12), channel_id=1, source_target_pairs={{0,8},{8,16},{16,24},{24,32},{32,40},{40,48},{48,56},{56,0},{1,9},... | collective-permute-start | bytes 294920 | tf_op jit(solution)/shard_map/ppermute | solution.py:27
  218.5 14.4 %collective-permute-start.5 = (f32[3,3,1,3,128]{4,2,3,1,0:T(1,128)S(1)}, f32[3,3,1,3,128]{4,2,3,1,0:T(1,128)S(1)}, u32[]{:S(2)}, u32[]{:S(2)}) collective-permute-start(f32[3,3,1,3,128]{4,2,3,1,0:T(1,128)S(1)} %pad_maximum_fusion.17), channel_id=1, source_target_pairs={{1,0},{2,1},{3,2},{4,3},{5,4},{6,5},{7,6},{0,7},{9,8},{10,9},{11,1... | collective-permute-start | bytes 41480 | tf_op jit(solution)/shard_map/ppermute | solution.py:28
  220.4 12.5 %collective-permute-start.4 = (f32[3,3,1,3,128]{4,2,3,1,0:T(1,128)S(1)}, f32[3,3,1,3,128]{4,2,3,1,0:T(1,128)S(1)}, u32[]{:S(2)}, u32[]{:S(2)}) collective-permute-start(f32[3,3,1,3,128]{4,2,3,1,0:T(1,128)S(1)} %pad_maximum_fusion.17), channel_id=1, source_target_pairs={{0,1},{1,2},{2,3},{3,4},{4,5},{5,6},{6,7},{7,0},{8,9},{9,10},{10,1... | collective-permute-start | bytes 41480 | tf_op jit(solution)/shard_map/ppermute | solution.py:27
  225.2 12.1 %collective-permute-start.11 = (bf16[3,3,1,128,128]{4,3,2,1,0:T(8,128)(2,1)S(1)}, bf16[3,3,1,128,128]{4,3,2,1,0:T(8,128)(2,1)S(1)}, u32[]{:S(2)}, u32[]{:S(2)}) collective-permute-start(bf16[3,3,1,128,128]{4,3,2,1,0:T(8,128)(2,1)S(1)} %pad_maximum_fusion.6), channel_id=1, source_target_pairs={{1,0},{2,1},{3,2},{4,3},{5,4},{6,5},{7,6},{0,7},{9,8},{10,9},{11,1... | collective-permute-start | bytes 884744 | tf_op jit(solution)/shard_map/ppermute | solution.py:28
  227.1 13.7 %collective-permute-start.10 = (bf16[3,3,1,128,128]{4,3,2,1,0:T(8,128)(2,1)S(1)}, bf16[3,3,1,128,128]{4,3,2,1,0:T(8,128)(2,1)S(1)}, u32[]{:S(2)}, u32[]{:S(2)}) collective-permute-start(bf16[3,3,1,128,128]{4,3,2,1,0:T(8,128)(2,1)S(1)} %pad_maximum_fusion.6), channel_id=1, source_target_pairs={{0,1},{1,2},{2,3},{3,4},{4,5},{5,6},{6,7},{7,0},{8,9},{9,10},{10,1... | collective-permute-start | bytes 884744 | tf_op jit(solution)/shard_map/ppermute | solution.py:27
  585.0 460.5 %all-reduce.9.cloned.1.call-start = ((), (), s32[]{:S(2)}) async-start(), calls=%async_computation | async-start | bytes 2097152 | tf_op jit(solution)/shard_map/psum | solution.py:185
  732.6 16.3 %collective-permute-start.13 = (bf16[1,1,1,128,128]{4,3,2,1,0:T(8,128)(2,1)S(1)}, bf16[1,1,1,128,128]{4,3,2,1,0:T(8,128)(2,1)S(1)}, u32[]{:S(2)}, u32[]{:S(2)}) collective-permute-start(bf16[1,1,1,128,128]{4,3,2,1,0:T(8,128)(2,1)S(1)} %bitcast.201), channel_id=1, source_target_pairs={{64,0},{128,64},{192,128},{256,192},{320,256},{384,320},{448,384},... | collective-permute-start | bytes 98312 | tf_op jit(solution)/shard_map/ppermute | solution.py:28
  735.8 13.1 %collective-permute-start.12 = (bf16[1,1,1,128,128]{4,3,2,1,0:T(8,128)(2,1)S(1)}, bf16[1,1,1,128,128]{4,3,2,1,0:T(8,128)(2,1)S(1)}, u32[]{:S(2)}, u32[]{:S(2)}) collective-permute-start(bf16[1,1,1,128,128]{4,3,2,1,0:T(8,128)(2,1)S(1)} %bitcast.202), channel_id=1, source_target_pairs={{0,64},{64,128},{128,192},{192,256},{256,320},{320,384},{384,448},... | collective-permute-start | bytes 98312 | tf_op jit(solution)/shard_map/ppermute | solution.py:27
  749.0 6.6 collective-permute-start.15
  751.1 5.5 collective-permute-start.14
  757.3 8.3 collective-permute-start.17
  759.9 11.7 %collective-permute-start.16 = (bf16[3,3,1,128,128]{4,3,2,1,0:T(8,128)(2,1)}, bf16[3,3,1,128,128]{4,3,2,1,0:T(8,128)(2,1)}, u32[]{:S(2)}, u32[]{:S(2)}) collective-permute-start(bf16[3,3,1,128,128]{4,3,2,1,0:T(8,128)(2,1)} %pad_maximum_fusion.7), channel_id=1, source_target_pairs={{0,1},{1,2},{2,3},{3,4},{4,5},{5,6},{6,7},{7,0},{8,9},{9,10},{10,1... | collective-permute-start | bytes 884744 | tf_op jit(solution)/shard_map/ppermute | solution.py:27
  (38 other events, 7976.9 us)
Sparse Core Ops, SparseCore 0:
  38.9 545.9 all-reduce.10
  588.0 129.9 all-reduce.12
  764.5 280.8 all-reduce.8
